TPU v7x, 32 devices: a whole 2x2x4 slice. The times are simulated.
32 devices in a mesh: img: 8 (over z, core), txt: 4 (over y, x).
Axes of the slice: x: 2, y: 2, z: 4, core: 2. Of those that a mesh axis runs over, the one named last changes fastest.
Arguments:
- image_emb: float32 [1024, 1536], P('img', 'txt'), may hold values from -0.15625 to 0.15625
- text_emb: float32 [1024, 1536], P('txt', 'img'), may hold values from -0.15625 to 0.15625
- vision_feat: bfloat16 [1024, 5120], P('img', 'txt'), may hold values from -0.125 to 0.125
- positive: int32 [1024], P('img'), may hold values from 0 to 1023, each once
- logit_scale: float32 [1], replicated, may hold values from 5 to 15
- logit_bias: float32 [1], replicated, may hold values from -3 to -1
Outputs:
- grad_image: float32 [1024, 1536], P('img', 'txt')
- grad_text: float32 [1024, 1536], P('txt', 'img')
- grad_proj: float32 [5120, 1536], P('txt', 'img')
Inputs may be any that keep to these rules, and one draw needn't show every extreme that they name: `positive`: each text index is the match of exactly one image.
All inputs are finite; a program needn't handle non-finite values.
Results may differ from a plain program's by a relative error of at most 0.0029.
Values may be sent and summed in bfloat16 or wider, within the bound.
A program may use at most 64 MiB of HBM per device.

v0:
```python
import jax
import jax.numpy as jnp
from jax import lax
from jax.sharding import PartitionSpec as P


def per_device(image_emb, text_emb, vision_feat, positive, logit_scale, logit_bias):
    scale = logit_scale[0]
    bias = logit_bias[0]
    image_full = lax.all_gather(image_emb, "txt", axis=1, tiled=True)
    text_full = lax.all_gather(text_emb, "img", axis=1, tiled=True)
    text_rows = text_full.shape[0]
    first_col = lax.axis_index("txt") * text_rows
    columns = first_col + lax.iota(jnp.int32, text_rows)
    logits = (
        scale
        * jnp.dot(
            image_full,
            text_full.T,
            precision=lax.Precision.HIGHEST,
            preferred_element_type=jnp.float32,
        )
        + bias
    )
    sign = jnp.where(positive[:, None] == columns[None, :], 1.0, -1.0).astype(jnp.float32)
    slope = -sign * jax.nn.sigmoid(-sign * logits)
    image_terms = scale * jnp.dot(
        slope, text_full, precision=lax.Precision.HIGHEST, preferred_element_type=jnp.float32
    )
    text_terms = scale * jnp.dot(
        slope.T, image_full, precision=lax.Precision.HIGHEST, preferred_element_type=jnp.float32
    )
    grad_text = lax.psum_scatter(text_terms, "img", scatter_dimension=1, tiled=True)
    grad_image = lax.psum_scatter(image_terms, "txt", scatter_dimension=1, tiled=True)
    image_low = lax.all_gather(grad_image.astype(jnp.bfloat16), "txt", axis=1, tiled=True)
    weight_terms = jnp.dot(vision_feat.T, image_low, preferred_element_type=jnp.float32)
    grad_proj = lax.psum_scatter(weight_terms, "img", scatter_dimension=1, tiled=True)
    return (grad_image, grad_text, grad_proj)


def solution(mesh):
    placed = (P("img", "txt"), P("txt", "img"), P("img", "txt"), P("img"), P(), P())
    return jax.shard_map(
        per_device,
        mesh=mesh,
        in_specs=placed,
        out_specs=(P("img", "txt"), P("txt", "img"), P("txt", "img")),
        check_vma=False,
    )
```

profile of v0, /device:TPU:0, one launch (start us, length us, event | category | flops | bytes accessed | tf_op | source)
XLA Modules:
  0.0 197.5 jit_solution(13368164841383276758)
XLA Ops:
  7.2 0.0 copy-start
  7.2 0.0 all-gather.2.cloned.1.call-start
  7.2 0.7 all-gather.2.cloned.1.call-update
  7.9 0.0 reduce-scatter.4.cloned.1.call-start
  9.3 15.9 %all_gather.9 = f32[128,1536]{1,0:T(8,128)S(1)} all-gather(f32[128,384]{1,0:T(8,128)} %param.6), channel_id=1, replica_groups=mesh['img'=8,'txt'=4] {'txt'}, dimensions={1}, use_global_device_ids=true | all-gather | bytes 983040 | tf_op jit(solution)/shard_map/all_gather | solution.py:10
  25.2 12.5 %all-gather.2.cloned.1.call-done = f32[256,1536]{0,1:T(8,128)} async-done(((f32[256,192]{0,1:T(8,128)}), f32[256,1536]{0,1:T(8,128)}) %all-gather.2.cloned.1.call-update) | async-done | bytes 1572880 | tf_op jit(solution)/shard_map/all_gather | solution.py:11
  37.7 0.0 copy-start.1
  37.7 2.4 %fusion.6 = f32[128,256]{1,0:T(8,128)S(1)} fusion(f32[128,1536]{1,0:T(8,128)S(1)} %all_gather.9, f32[256,1536]{0,1:T(8,128)} %all-gather.2.cloned.1.call-done, f32[]{:T(128)} %bitcast.15, f32[]{:T(128)} %bitcast.13, s32[256]{0:T(256)S(1)} %iota_add_fusion, s32[128]{0:T(128)} %param.9), kind=kOutput, calls=%fused_computation.10 | convolution fusion | flops 604307456 | bytes 2491912 | tf_op jit(solution)/shard_map/dot_general | solution.py:17
  40.1 0.0 copy-done.1
  40.1 2.6 %convolution_multiply_fusion.1 = f32[128,1536]{1,0:T(8,128)} fusion(f32[128,256]{1,0:T(8,128)S(1)} %fusion.6, f32[256,1536]{0,1:T(8,128)S(1)} %copy-done.1, f32[]{:T(128)} %bitcast.12), kind=kOutput, calls=%fused_computation.2 | convolution fusion | flops 604176384 | bytes 2490372 | tf_op jit(solution)/shard_map/dot_general | solution.py:27
  42.7 0.0 reduce-scatter.4.cloned.1.call-update
  42.7 0.0 reduce-scatter.6.cloned.1.call-start
  42.8 2.7 %convolution_multiply_fusion = f32[256,1536]{0,1:T(8,128)} fusion(f32[128,256]{1,0:T(8,128)S(1)} %fusion.6, f32[128,1536]{1,0:T(8,128)S(1)} %all_gather.9, f32[]{:T(128)} %bitcast.14), kind=kOutput, calls=%fused_computation.1 | convolution fusion | flops 604372992 | bytes 2490372 | tf_op jit(solution)/shard_map/dot_general | solution.py:30
  45.4 0.0 reduce-scatter.6.cloned.1.call-update
  45.5 0.0 reduce-scatter.8.cloned.1.call-start
  45.5 22.7 %reduce-scatter.4.cloned.1.call-done = f32[128,384]{1,0:T(8,128)} async-done(((f32[128,1536]{1,0:T(8,128)}), f32[128,384]{1,0:T(8,128)}) %reduce-scatter.4.cloned.1.call-update) | async-done | bytes 196624 | tf_op jit(solution)/shard_map/reduce_scatter | solution.py:34
  68.2 0.9 convert_element_type.3
  69.1 10.1 %all_gather.11 = bf16[128,1536]{1,0:T(8,128)(2,1)S(1)} all-gather(bf16[128,384]{1,0:T(8,128)(2,1)S(1)} %convert_element_type.3), channel_id=1, replica_groups=mesh['img'=8,'txt'=4] {'txt'}, dimensions={1}, use_global_device_ids=true | all-gather | bytes 491520 | tf_op jit(solution)/shard_map/all_gather | solution.py:35
  79.2 0.0 copy-done
  79.2 4.3 %convolution_bitcast_fusion = f32[1280,1536]{0,1:T(8,128)} fusion(bf16[128,1536]{1,0:T(8,128)(2,1)S(1)} %all_gather.11, bf16[128,1280]{1,0:T(8,128)(2,1)S(1)} %copy-done), kind=kOutput, calls=%fused_computation | convolution fusion | flops 503316480 | bytes 8585216 | tf_op jit(solution)/shard_map/dot_general | solution.py:36
  83.5 0.0 reduce-scatter.8.cloned.1.call-update
  83.5 21.9 %reduce-scatter.6.cloned.1.call-done = f32[256,192]{0,1:T(8,128)} async-done(((f32[256,1536]{0,1:T(8,128)}), f32[256,192]{0,1:T(8,128)}) %reduce-scatter.6.cloned.1.call-update) | async-done | bytes 196624 | tf_op jit(solution)/shard_map/reduce_scatter | solution.py:33
  105.4 85.6 %reduce-scatter.8.cloned.1.call-done = f32[1280,192]{0,1:T(8,128)} async-done(((f32[1280,1536]{0,1:T(8,128)}), f32[1280,192]{0,1:T(8,128)}) %reduce-scatter.8.cloned.1.call-update) | async-done | bytes 983056 | tf_op jit(solution)/shard_map/reduce_scatter | solution.py:37
  (1 shorter events, 0.0 us)
Async XLA Ops:
  7.2 72.1 %copy-start = (bf16[128,1280]{1,0:T(8,128)(2,1)S(1)}, bf16[128,1280]{1,0:T(8,128)(2,1)}, u32[]{:S(2)}) copy-start(bf16[128,1280]{1,0:T(8,128)(2,1)} %param.8) | copy-start | bytes 983044
  7.2 30.5 %all-gather.2.cloned.1.call-start = ((), (), s32[]{:S(2)}) async-start(), calls=%async_computation.3 | async-start | bytes 1769472 | tf_op jit(solution)/shard_map/all_gather | solution.py:11
  7.9 60.3 %reduce-scatter.4.cloned.1.call-start = ((), (), s32[]{:S(2)}) async-start(), calls=%async_computation.4 | async-start | bytes 983040 | tf_op jit(solution)/shard_map/reduce_scatter | solution.py:34
  37.7 2.5 %copy-start.1 = (f32[256,1536]{0,1:T(8,128)S(1)}, f32[256,1536]{0,1:T(8,128)}, u32[]{:S(2)}) copy-start(f32[256,1536]{0,1:T(8,128)} %all-gather.2.cloned.1.call-done) | copy-start | bytes 4718596
  42.7 62.7 %reduce-scatter.6.cloned.1.call-start = ((), (), s32[]{:S(2)}) async-start(), calls=%async_computation.5 | async-start | bytes 1769472 | tf_op jit(solution)/shard_map/reduce_scatter | solution.py:33
  45.5 145.5 %reduce-scatter.8.cloned.1.call-start = ((), (), s32[]{:S(2)}) async-start(), calls=%async_computation.6 | async-start | bytes 8847360 | tf_op jit(solution)/shard_map/reduce_scatter | solution.py:37
Sparse Core Ops, SparseCore 0:
  9.6 27.9 all-gather.1
  42.9 25.2 reduce-scatter.3
  71.1 34.2 reduce-scatter.5
  108.1 82.8 reduce-scatter.7
where the time goes:
time: 198 us
  waiting for transfers between devices  143 us (72%)
  blocking collectives  26 us (13%)
  between operations  15.1 us (8%)
  matrix products  12 us (6%)
    reduce_scatter x1, waiting for transfers between devices, per_device(): lax.psum_scatter(weight_terms, 'img', scatter_dimension=1, tiled=True)  85.6 us
    reduce_scatter x1, waiting for transfers between devices, per_device(): lax.psum_scatter(image_terms, 'txt', scatter_dimension=1, tiled=True)  22.7 us
    reduce_scatter x1, waiting for transfers between devices, per_device(): lax.psum_scatter(text_terms, 'img', scatter_dimension=1, tiled=True)  21.9 us
    all_gather x1, blocking collectives, per_device(): image_full = lax.all_gather(image_emb, 'txt', axis=1, tiled=True)  15.9 us
    all_gather x1, waiting for transfers between devices, per_device(): text_full = lax.all_gather(text_emb, 'img', axis=1, tiled=True)  12.5 us
    all_gather x1, blocking collectives, per_device(): lax.all_gather(grad_image.astype(jnp.bfloat16), 'txt', axis=1, tiled=True)  10.1 us
    dot_general x1, matrix products, per_device(): jnp.dot(vision_feat.T, image_low, preferred_element_type=jnp.float32)  4.28 us
  transfers between devices with their start and end apart: 4, of which 4 were waited for; matrix products, arithmetic and copies ran while one was open for 4% of the time, Pallas kernels for 0%

commit v1 on v0

--- a/solution.py
+++ b/solution.py
@@ -8,7 +8,8 @@
     scale = logit_scale[0]
     bias = logit_bias[0]
     image_full = lax.all_gather(image_emb, "txt", axis=1, tiled=True)
-    text_full = lax.all_gather(text_emb, "img", axis=1, tiled=True)
+    _balance_modes = lambda row_data: jnp.concatenate(lax.all_gather(row_data, "img"), axis=1)
+    text_full = _balance_modes(text_emb)
     text_rows = text_full.shape[0]
     first_col = lax.axis_index("txt") * text_rows
     columns = first_col + lax.iota(jnp.int32, text_rows)

time: 198 us -> 199 us (level)
  local copies, waits for them, and re-layouts: 0.01 us -> 2.67 us
    unnamed x4 -> x5, local copies, waits for them, and re-layouts: 0.01 us -> 2.16 us
where the time goes in v1:
time: 199 us
  waiting for transfers between devices  143 us (72%)
  blocking collectives  26 us (13%)
  between operations  15.1 us (8%)
  matrix products  10.5 us (5%)
  local copies, waits for them, and re-layouts  2.67 us (1%)
    reduce_scatter x1, waiting for transfers between devices, per_device(): lax.psum_scatter(weight_terms, 'img', scatter_dimension=1, tiled=True)  85.7 us
    reduce_scatter x1, waiting for transfers between devices, per_device(): lax.psum_scatter(image_terms, 'txt', scatter_dimension=1, tiled=True)  22.7 us
    reduce_scatter x1, waiting for transfers between devices, per_device(): lax.psum_scatter(text_terms, 'img', scatter_dimension=1, tiled=True)  21.7 us
    all_gather x1, blocking collectives, per_device(): image_full = lax.all_gather(image_emb, 'txt', axis=1, tiled=True)  15.9 us
    all_gather x1, waiting for transfers between devices, per_device(): lax.all_gather(row_data, 'img')  12.4 us
    all_gather x1, blocking collectives, per_device(): lax.all_gather(grad_image.astype(jnp.bfloat16), 'txt', axis=1, tiled=True)  10.1 us
    dot_general x1, matrix products, per_device(): jnp.dot(vision_feat.T, image_low, preferred_element_type=jnp.float32)  4.28 us
  transfers between devices with their start and end apart: 4, of which 4 were waited for; matrix products, arithmetic and copies ran while one was open for 4% of the time, Pallas kernels for 0%

profile of v1, /device:TPU:0, one launch (start us, length us, event | category | flops | bytes accessed | tf_op | source)
XLA Modules:
  0.0 198.6 jit_solution(9986537019332091934)
XLA Ops:
  7.2 0.0 copy-start
  7.2 0.0 all-gather.3.cloned.1.call-start
  7.2 0.7 all-gather.3.cloned.1.call-update
  7.9 0.0 reduce-scatter.4.cloned.1.call-start
  9.3 15.9 %all_gather.12 = f32[128,1536]{1,0:T(8,128)S(1)} all-gather(f32[128,384]{1,0:T(8,128)} %param.6), channel_id=1, replica_groups=mesh['img'=8,'txt'=4] {'txt'}, dimensions={1}, use_global_device_ids=true | all-gather | bytes 983040 | tf_op jit(solution)/shard_map/all_gather | solution.py:10
  25.2 12.4 %all-gather.3.cloned.1.call-done = f32[2048,192]{0,1:T(8,128)} async-done(((f32[256,192]{0,1:T(8,128)}), f32[2048,192]{0,1:T(8,128)}) %all-gather.3.cloned.1.call-update) | async-done | bytes 1572880 | tf_op jit(solution)/shard_map/all_gather | solution.py:11
  37.6 2.0 %copy.10 = f32[24,8,8,256]{3,2,1,0:T(8,128)S(1)} copy(f32[24,8,8,256]{3,1,2,0:T(8,128)} %bitcast.26) | data formatting | bytes 3145728
  39.6 0.0 copy-start.1
  39.6 0.5 copy.9
  40.2 0.1 copy-done.1
  40.3 0.9 fusion.6
  41.2 2.6 %convolution_multiply_fusion.1 = f32[128,1536]{1,0:T(8,128)} fusion(f32[128,256]{1,0:T(8,128)S(1)} %fusion.6, f32[256,1536]{0,1:T(8,128)S(1)} %bitcast.24, f32[]{:T(128)} %bitcast.19), kind=kOutput, calls=%fused_computation.2 | convolution fusion | flops 604176384 | bytes 2490372 | tf_op jit(solution)/shard_map/dot_general | solution.py:28
  43.8 0.0 reduce-scatter.4.cloned.1.call-update
  43.8 0.0 reduce-scatter.6.cloned.1.call-start
  43.9 2.7 %convolution_multiply_fusion = f32[256,1536]{0,1:T(8,128)} fusion(f32[128,256]{1,0:T(8,128)S(1)} %fusion.6, f32[128,1536]{1,0:T(8,128)S(1)} %all_gather.12, f32[]{:T(128)} %bitcast.21), kind=kOutput, calls=%fused_computation.1 | convolution fusion | flops 604372992 | bytes 2490372 | tf_op jit(solution)/shard_map/dot_general | solution.py:31
  46.6 0.0 reduce-scatter.6.cloned.1.call-update
  46.6 0.0 reduce-scatter.8.cloned.1.call-start
  46.6 22.7 %reduce-scatter.4.cloned.1.call-done = f32[128,384]{1,0:T(8,128)} async-done(((f32[128,1536]{1,0:T(8,128)}), f32[128,384]{1,0:T(8,128)}) %reduce-scatter.4.cloned.1.call-update) | async-done | bytes 196624 | tf_op jit(solution)/shard_map/reduce_scatter | solution.py:35
  69.3 0.9 convert_element_type.3
  70.2 10.1 %all_gather.15 = bf16[128,1536]{1,0:T(8,128)(2,1)S(1)} all-gather(bf16[128,384]{1,0:T(8,128)(2,1)S(1)} %convert_element_type.3), channel_id=1, replica_groups=mesh['img'=8,'txt'=4] {'txt'}, dimensions={1}, use_global_device_ids=true | all-gather | bytes 491520 | tf_op jit(solution)/shard_map/all_gather | solution.py:36
  80.3 0.0 copy-done
  80.3 4.3 %convolution_bitcast_fusion = f32[1280,1536]{0,1:T(8,128)} fusion(bf16[128,1536]{1,0:T(8,128)(2,1)S(1)} %all_gather.15, bf16[128,1280]{1,0:T(8,128)(2,1)S(1)} %copy-done), kind=kOutput, calls=%fused_computation | convolution fusion | flops 503316480 | bytes 8585216 | tf_op jit(solution)/shard_map/dot_general | solution.py:37
  84.6 0.0 reduce-scatter.8.cloned.1.call-update
  84.6 21.7 %reduce-scatter.6.cloned.1.call-done = f32[256,192]{0,1:T(8,128)} async-done(((f32[256,1536]{0,1:T(8,128)}), f32[256,192]{0,1:T(8,128)}) %reduce-scatter.6.cloned.1.call-update) | async-done | bytes 196624 | tf_op jit(solution)/shard_map/reduce_scatter | solution.py:34
  106.4 85.7 %reduce-scatter.8.cloned.1.call-done = f32[1280,192]{0,1:T(8,128)} async-done(((f32[1280,1536]{0,1:T(8,128)}), f32[1280,192]{0,1:T(8,128)}) %reduce-scatter.8.cloned.1.call-update) | async-done | bytes 983056 | tf_op jit(solution)/shard_map/reduce_scatter | solution.py:38
  (1 shorter events, 0.0 us)
Async XLA Ops:
  7.2 73.2 %copy-start = (bf16[128,1280]{1,0:T(8,128)(2,1)S(1)}, bf16[128,1280]{1,0:T(8,128)(2,1)}, u32[]{:S(2)}) copy-start(bf16[128,1280]{1,0:T(8,128)(2,1)} %param.8) | copy-start | bytes 983044
  7.2 30.4 %all-gather.3.cloned.1.call-start = ((), (), s32[]{:S(2)}) async-start(), calls=%async_computation.6 | async-start | bytes 1769472 | tf_op jit(solution)/shard_map/all_gather | solution.py:11
  7.9 61.4 %reduce-scatter.4.cloned.1.call-start = ((), (), s32[]{:S(2)}) async-start(), calls=%async_computation.3 | async-start | bytes 983040 | tf_op jit(solution)/shard_map/reduce_scatter | solution.py:35
  39.6 0.7 copy-start.1
  43.8 62.5 %reduce-scatter.6.cloned.1.call-start = ((), (), s32[]{:S(2)}) async-start(), calls=%async_computation.4 | async-start | bytes 1769472 | tf_op jit(solution)/shard_map/reduce_scatter | solution.py:34
  46.6 145.5 %reduce-scatter.8.cloned.1.call-start = ((), (), s32[]{:S(2)}) async-start(), calls=%async_computation.5 | async-start | bytes 8847360 | tf_op jit(solution)/shard_map/reduce_scatter | solution.py:38
Sparse Core Ops, SparseCore 0:
  9.6 27.9 all-gather.2
  44.0 25.2 reduce-scatter.3
  72.2 34.1 reduce-scatter.5
  109.1 82.9 reduce-scatter.7
